TPU v7x, 32 devices: a whole 2x2x4 slice. The times are simulated.
32 devices in a mesh: seqa: 4 (over x, core), seqb: 8 (over z, y).
Axes of the slice: x: 2, y: 2, z: 4, core: 2. Of those that a mesh axis runs over, the one named last changes fastest.
Arguments:
- sequence_input: bfloat16 [16384, 640], P(('seqa', 'seqb')), may hold values from -6 to 6
- w_prev: bfloat16 [3, 640, 1280], P(None, 'seqa'), may hold values from -0.15625 to 0.15625
- w_now: bfloat16 [3, 640, 1280], P(None, 'seqa'), may hold values from -0.15625 to 0.15625
- conv_bias: float32 [3, 1280], replicated, may hold values from -4 to 4
- w_mix: bfloat16 [3, 640, 640], P(None, None, 'seqa'), may hold values from -0.25 to 0.25
Outputs:
- seq_out: bfloat16 [16384, 640], P(('seqa', 'seqb'))
All inputs are finite; a program needn't handle non-finite values.
Results may differ from a plain program's by a relative error of at most 0.0052.
Values may be sent and summed in bfloat16 or wider, within the bound.
A program may use at most 64 MiB of HBM per device.

v0:
```python
import jax
import jax.numpy as jnp
from jax import lax
from jax.sharding import PartitionSpec as P

D = 640
DILATION_FIRST1 = 128
DILATION_SECOND2 = 512
DILATION_THIRD3 = 2048


def from_behind(value, axis, by):
    peers = lax.axis_size(axis)
    pairs = [(i, i + by) for i in range(peers) if 0 <= i + by < peers]
    return lax.ppermute(value, axis, pairs)


def norm_rows(values):
    scale = lax.rsqrt(jnp.mean(values * values, axis=1, keepdims=True) + 1e-06)
    return (values * scale).astype(jnp.bfloat16)


def block_prior(normed, dilation_step):
    rows = normed.shape[0]
    whole = dilation_step // rows
    part = dilation_step % rows
    pieces = []
    if part > 0:
        pieces.append(from_behind(normed[rows - part :], ("seqa", "seqb"), whole + 1))
    head = normed[: rows - part]
    if whole > 0:
        head = from_behind(head, ("seqa", "seqb"), whole)
    pieces.append(head)
    return jnp.concatenate(pieces, axis=0)


def one_layer(hidden_state, tap_prev, tap_now, bias, mixing, dilation_step):
    normed = norm_rows(hidden_state)
    earlier = block_prior(normed, dilation_step)
    rows = hidden_state.shape[0]
    start_sum = jnp.broadcast_to(bias[None, :], (rows, bias.shape[0]))
    total = start_sum
    total = total + jnp.dot(
        earlier,
        lax.all_gather(tap_prev, "seqa", axis=0, tiled=True),
        preferred_element_type=jnp.float32,
    )
    pre = total + jnp.dot(
        normed,
        lax.all_gather(tap_now, "seqa", axis=0, tiled=True),
        preferred_element_type=jnp.float32,
    )
    hidden = (pre[:, :D] * jax.nn.sigmoid(pre[:, D:])).astype(jnp.bfloat16)
    return hidden_state + jnp.dot(
        hidden,
        lax.all_gather(mixing, "seqa", axis=1, tiled=True),
        preferred_element_type=jnp.float32,
    )


def local(sequence_input, w_prev, w_now, conv_bias, w_mix):
    hidden_state = sequence_input.astype(jnp.float32)
    for layer_index, dilation_step in enumerate(
        (DILATION_FIRST1, DILATION_SECOND2, DILATION_THIRD3)
    ):
        hidden_state = one_layer(
            hidden_state,
            w_prev[layer_index],
            w_now[layer_index],
            conv_bias[layer_index],
            w_mix[layer_index],
            dilation_step,
        )
    block_output = hidden_state.astype(jnp.bfloat16)
    return block_output


def solution(mesh):
    return jax.shard_map(
        local,
        mesh=mesh,
        in_specs=(
            P(("seqa", "seqb"), None),
            P(None, "seqa", None),
            P(None, "seqa", None),
            P(),
            P(None, None, "seqa"),
        ),
        out_specs=P(("seqa", "seqb"), None),
        check_vma=False,
    )
```

profile of v0, /device:TPU:0, one launch (start us, length us, event | category | flops | bytes accessed | tf_op | source)
XLA Modules:
  0.0 173.4 jit_solution(16757699871526327815)
XLA Ops:
  6.5 2.4 %fusion.47 = (bf16[1,160,1280]{2,1,0:T(8,128)(2,1)}, bf16[1,160,1280]{2,1,0:T(8,128)(2,1)}, bf16[1,160,1280]{2,1,0:T(8,128)(2,1)}) fusion(bf16[3,160,1280]{2,1,0:T(8,128)(2,1)} %param.7), kind=kLoop, calls=%fused_computation.65 | loop fusion | bytes 2457600 | tf_op jit(solution)/shard_map/slice | solution.py:69
  9.1 1.1 fusion.46
  13.3 5.6 %collective-permute-start = (bf16[128,640]{1,0:T(8,128)(2,1)}, bf16[128,640]{1,0:T(8,128)(2,1)}, u32[]{:S(2)}, u32[]{:S(2)}) collective-permute-start(bf16[128,640]{1,0:T(8,128)(2,1)} %slice.80), channel_id=1, source_target_pairs={{0,1},{1,2},{2,3},{3,4},{4,5},{5,6},{6,7},{7,8},{8,9},{9,10},{10,1... | collective-permute-start | bytes 491528 | tf_op jit(solution)/shard_map/ppermute | solution.py:15
  20.5 13.9 %all-gather.2 = bf16[1,640,640]{1,2,0:T(8,128)(2,1)} all-gather(bf16[1,640,160]{1,2,0:T(8,128)(2,1)S(1)} %get-tuple-element.15), channel_id=4, replica_groups=mesh['seqa'=4,'seqb'=8] {'seqa'}, dimensions={2}, use_global_device_ids=true | all-gather | bytes 1024000 | tf_op jit(solution)/shard_map/all_gather | solution.py:56
  34.4 1.9 %all-gather.18.cloned.1.call-done = bf16[1,640,1280]{2,1,0:T(8,128)(2,1)} async-done(((bf16[1,160,1280]{2,1,0:T(8,128)(2,1)}), bf16[1,640,1280]{2,1,0:T(8,128)(2,1)}) %all-gather.18.cloned.1.call-update) | async-done | bytes 1638416 | tf_op jit(solution)/shard_map/all_gather | solution.py:50
  36.3 2.8 %fusion.9 = f32[512,1280]{1,0:T(8,128)S(1)} fusion(bf16[512,640]{1,0:T(8,128)(2,1)} %copy-done.1, bf16[1,640,1280]{2,1,0:T(8,128)(2,1)} %all-gather.18.cloned.1.call-done), kind=kOutput, calls=%fused_computation.15 | convolution fusion | flops 838860800 | bytes 4915200 | tf_op jit(solution)/shard_map/dot_general | solution.py:48
  39.1 18.8 %all-gather.16.cloned.1.call-done = bf16[1,640,1280]{2,1,0:T(8,128)(2,1)} async-done(((bf16[1,160,1280]{2,1,0:T(8,128)(2,1)}), bf16[1,640,1280]{2,1,0:T(8,128)(2,1)}) %all-gather.16.cloned.1.call-update) | async-done | bytes 1638416 | tf_op jit(solution)/shard_map/all_gather | solution.py:45
  57.9 2.9 %fusion = f32[512,1280]{1,0:T(8,128)S(1)} fusion(f32[512,1280]{1,0:T(8,128)S(1)} %fusion.9, bf16[1,640,1280]{2,1,0:T(8,128)(2,1)} %all-gather.16.cloned.1.call-done, f32[1280]{0:T(1024)S(1)} %get-tuple-element.6, bf16[384,640]{1,0:T(8,128)(2,1)} %slice.81, bf16[128,640]{1,0:T(8,128)(2,1)} %collective-permute-done), kind=kOutput, calls=%fused_computation.3 | convolution fusion | flops 841482240 | bytes 7541760 | tf_op jit(solution)/shard_map/dot_general | solution.py:43
  61.8 1.0 copy-done.4
  63.8 4.3 %collective-permute-start.1 = (bf16[512,640]{1,0:T(8,128)(2,1)}, bf16[512,640]{1,0:T(8,128)(2,1)}, u32[]{:S(2)}, u32[]{:S(2)}) collective-permute-start(bf16[512,640]{1,0:T(8,128)(2,1)} %multiply_convert_fusion.1), channel_id=1, source_target_pairs={{0,1},{1,2},{2,3},{3,4},{4,5},{5,6},{6,7},{7,8},{8,9},{9,10},{10,1... | collective-permute-start | bytes 1966088 | tf_op jit(solution)/shard_map/ppermute | solution.py:15
  68.1 13.7 %all-gather.5 = bf16[1,640,640]{1,2,0:T(8,128)(2,1)} all-gather(bf16[1,640,160]{1,2,0:T(8,128)(2,1)S(1)} %copy-done.7), channel_id=7, replica_groups=mesh['seqa'=4,'seqb'=8] {'seqa'}, dimensions={2}, use_global_device_ids=true | all-gather | bytes 1024000 | tf_op jit(solution)/shard_map/all_gather | solution.py:56
  81.8 2.1 %all-gather.22.cloned.1.call-done = bf16[1,640,1280]{2,1,0:T(8,128)(2,1)} async-done(((bf16[1,160,1280]{2,1,0:T(8,128)(2,1)}), bf16[1,640,1280]{2,1,0:T(8,128)(2,1)}) %all-gather.22.cloned.1.call-update) | async-done | bytes 1638416 | tf_op jit(solution)/shard_map/all_gather | solution.py:50
  83.9 2.8 %fusion.6 = f32[512,1280]{1,0:T(8,128)S(1)} fusion(bf16[512,640]{1,0:T(8,128)(2,1)} %multiply_convert_fusion.1, bf16[1,640,1280]{2,1,0:T(8,128)(2,1)} %all-gather.22.cloned.1.call-done), kind=kOutput, calls=%fused_computation.12 | convolution fusion | flops 838860800 | bytes 4915200 | tf_op jit(solution)/shard_map/dot_general | solution.py:48
  86.7 22.9 %all-gather.20.cloned.1.call-done = bf16[1,640,1280]{2,1,0:T(8,128)(2,1)} async-done(((bf16[1,160,1280]{2,1,0:T(8,128)(2,1)}), bf16[1,640,1280]{2,1,0:T(8,128)(2,1)}) %all-gather.20.cloned.1.call-update) | async-done | bytes 1638416 | tf_op jit(solution)/shard_map/all_gather | solution.py:45
  109.6 3.0 %fusion.1 = f32[512,1280]{1,0:T(8,128)S(1)} fusion(f32[512,1280]{1,0:T(8,128)S(1)} %fusion.6, bf16[512,640]{1,0:T(8,128)(2,1)} %collective-permute-done.1, bf16[1,640,1280]{2,1,0:T(8,128)(2,1)} %all-gather.20.cloned.1.call-done, f32[1280]{0:T(1024)S(1)} %get-tuple-element.7), kind=kOutput, calls=%fused_computation.4 | convolution fusion | flops 840171520 | bytes 7541760 | tf_op jit(solution)/shard_map/dot_general | solution.py:43
  112.6 1.0 multiply_reduce_fusion
  113.6 1.1 copy-done.2
  115.6 4.3 %collective-permute-start.2 = (bf16[512,640]{1,0:T(8,128)(2,1)}, bf16[512,640]{1,0:T(8,128)(2,1)S(1)}, u32[]{:S(2)}, u32[]{:S(2)}) collective-permute-start(bf16[512,640]{1,0:T(8,128)(2,1)} %multiply_convert_fusion), channel_id=1, source_target_pairs={{0,4},{1,5},{2,6},{3,7},{4,8},{5,9},{6,10},{7,11},{8,12},{9,13},{1... | collective-permute-start | bytes 1966088 | tf_op jit(solution)/shard_map/ppermute | solution.py:15
  120.0 14.0 %all-gather.8 = bf16[1,640,640]{1,2,0:T(8,128)(2,1)} all-gather(bf16[1,640,160]{1,2,0:T(8,128)(2,1)S(1)} %get-tuple-element.14), channel_id=10, replica_groups=mesh['seqa'=4,'seqb'=8] {'seqa'}, dimensions={2}, use_global_device_ids=true | all-gather | bytes 1024000 | tf_op jit(solution)/shard_map/all_gather | solution.py:56
  134.0 1.4 all-gather.26.cloned.1.call-done
  135.4 2.8 %fusion.3 = f32[512,1280]{1,0:T(8,128)S(1)} fusion(bf16[512,640]{1,0:T(8,128)(2,1)} %multiply_convert_fusion, bf16[1,640,1280]{2,1,0:T(8,128)(2,1)} %all-gather.26.cloned.1.call-done), kind=kOutput, calls=%fused_computation.9 | convolution fusion | flops 838860800 | bytes 4915200 | tf_op jit(solution)/shard_map/dot_general | solution.py:48
  138.2 23.8 %all-gather.24.cloned.1.call-done = bf16[1,640,1280]{2,1,0:T(8,128)(2,1)} async-done(((bf16[1,160,1280]{2,1,0:T(8,128)(2,1)}), bf16[1,640,1280]{2,1,0:T(8,128)(2,1)}) %all-gather.24.cloned.1.call-update) | async-done | bytes 1638416 | tf_op jit(solution)/shard_map/all_gather | solution.py:45
  162.0 2.8 %fusion.2 = f32[512,1280]{1,0:T(8,128)S(1)} fusion(f32[512,1280]{1,0:T(8,128)S(1)} %fusion.3, bf16[512,640]{1,0:T(8,128)(2,1)S(1)} %collective-permute-done.2, bf16[1,640,1280]{2,1,0:T(8,128)(2,1)} %all-gather.24.cloned.1.call-done, f32[1280]{0:T(1024)S(1)} %get-tuple-element.5), kind=kOutput, calls=%fused_computation.5 | convolution fusion | flops 840171520 | bytes 7541760 | tf_op jit(solution)/shard_map/dot_general | solution.py:43
  164.8 1.7 fusion.12
  (51 shorter events, 7.7 us)
Async XLA Ops:
  6.5 2.5 %copy-start.6 = (bf16[3,160,1280]{2,1,0:T(8,128)(2,1)S(1)}, bf16[3,160,1280]{2,1,0:T(8,128)(2,1)}, u32[]{:S(2)}) copy-start(bf16[3,160,1280]{2,1,0:T(8,128)(2,1)} %param.6) | copy-start | bytes 3686404
  6.5 29.7 %all-gather.18.cloned.1.call-start = ((), (), s32[]{:S(2)}) async-start(), calls=%async_computation.1 | async-start | bytes 2048000 | tf_op jit(solution)/shard_map/all_gather | solution.py:50
  9.0 48.9 %all-gather.16.cloned.1.call-start = ((), (), s32[]{:S(2)}) async-start(), calls=%async_computation | async-start | bytes 2048000 | tf_op jit(solution)/shard_map/all_gather | solution.py:45
  10.2 2.0 %copy-start = (bf16[512,640]{1,0:T(8,128)(2,1)S(1)}, bf16[512,640]{1,0:T(8,128)(2,1)}, u32[]{:S(2)}) copy-start(bf16[512,640]{1,0:T(8,128)(2,1)} %param.5) | copy-start | bytes 1966084
  10.2 73.7 %all-gather.22.cloned.1.call-start = ((), (), s32[]{:S(2)}) async-start(), calls=%async_computation.3 | async-start | bytes 2048000 | tf_op jit(solution)/shard_map/all_gather | solution.py:50
  10.9 98.6 %all-gather.20.cloned.1.call-start = ((), (), s32[]{:S(2)}) async-start(), calls=%async_computation.2 | async-start | bytes 2048000 | tf_op jit(solution)/shard_map/all_gather | solution.py:45
  11.5 123.9 %all-gather.26.cloned.1.call-start = ((), (), s32[]{:S(2)}) async-start(), calls=%async_computation.5 | async-start | bytes 2048000 | tf_op jit(solution)/shard_map/all_gather | solution.py:50
  12.1 149.9 %all-gather.24.cloned.1.call-start = ((), (), s32[]{:S(2)}) async-start(), calls=%async_computation.4 | async-start | bytes 2048000 | tf_op jit(solution)/shard_map/all_gather | solution.py:45
  12.4 7.4 %copy-start.12 = (f32[3,1280]{1,0:T(4,128)S(1)}, f32[3,1280]{1,0:T(4,128)}, u32[]{:S(2)}) copy-start(f32[3,1280]{1,0:T(4,128)} %param.8) | copy-start | bytes 46084
  12.4 7.4 %copy-start.11 = (bf16[3,640,160]{1,2,0:T(8,128)(2,1)S(1)}, bf16[3,640,160]{1,2,0:T(8,128)(2,1)}, u32[]{:S(2)}) copy-start(bf16[3,640,160]{1,2,0:T(8,128)(2,1)} %param.9) | copy-start | bytes 1843204
  12.6 8.0 %copy-start.1 = (bf16[512,640]{1,0:T(8,128)(2,1)}, bf16[512,640]{1,0:T(8,128)(2,1)S(1)}, u32[]{:S(2)}) copy-start(bf16[512,640]{1,0:T(8,128)(2,1)S(1)} %fusion.14) | copy-start | bytes 1966084
  13.3 25.8 %collective-permute-start = (bf16[128,640]{1,0:T(8,128)(2,1)}, bf16[128,640]{1,0:T(8,128)(2,1)}, u32[]{:S(2)}, u32[]{:S(2)}) collective-permute-start(bf16[128,640]{1,0:T(8,128)(2,1)} %slice.80), channel_id=1, source_target_pairs={{0,1},{1,2},{2,3},{3,4},{4,5},{5,6},{6,7},{7,8},{8,9},{9,10},{10,1... | collective-permute-start | bytes 491528 | tf_op jit(solution)/shard_map/ppermute | solution.py:15
  57.9 2.9 %copy-start.8 = (bf16[1,640,640]{1,2,0:T(8,128)(2,1)S(1)}, bf16[1,640,640]{1,2,0:T(8,128)(2,1)}, u32[]{:S(2)}) copy-start(bf16[1,640,640]{1,2,0:T(8,128)(2,1)} %all-gather.2) | copy-start | bytes 2457604
  61.8 1.1 copy-start.4
  61.8 6.3 %copy-start.7 = (bf16[1,640,160]{1,2,0:T(8,128)(2,1)S(1)}, bf16[1,640,160]{1,2,0:T(8,128)(2,1)}, u32[]{:S(2)}) copy-start(bf16[1,640,160]{1,2,0:T(8,128)(2,1)} %get-tuple-element.16) | copy-start | bytes 614404
  63.8 45.7 %collective-permute-start.1 = (bf16[512,640]{1,0:T(8,128)(2,1)}, bf16[512,640]{1,0:T(8,128)(2,1)}, u32[]{:S(2)}, u32[]{:S(2)}) collective-permute-start(bf16[512,640]{1,0:T(8,128)(2,1)} %multiply_convert_fusion.1), channel_id=1, source_target_pairs={{0,1},{1,2},{2,3},{3,4},{4,5},{5,6},{6,7},{7,8},{8,9},{9,10},{10,1... | collective-permute-start | bytes 1966088 | tf_op jit(solution)/shard_map/ppermute | solution.py:15
  109.6 3.0 %copy-start.5 = (f32[512,640]{1,0:T(8,128)S(1)}, f32[512,640]{1,0:T(8,128)}, u32[]{:S(2)}) copy-start(f32[512,640]{1,0:T(8,128)} %copy-done.4) | copy-start | bytes 3932164
  109.6 3.0 %copy-start.9 = (bf16[1,640,640]{1,2,0:T(8,128)(2,1)S(1)}, bf16[1,640,640]{1,2,0:T(8,128)(2,1)}, u32[]{:S(2)}) copy-start(bf16[1,640,640]{1,2,0:T(8,128)(2,1)} %all-gather.5) | copy-start | bytes 2457604
  113.5 1.1 copy-start.2
  115.6 46.4 %collective-permute-start.2 = (bf16[512,640]{1,0:T(8,128)(2,1)}, bf16[512,640]{1,0:T(8,128)(2,1)S(1)}, u32[]{:S(2)}, u32[]{:S(2)}) collective-permute-start(bf16[512,640]{1,0:T(8,128)(2,1)} %multiply_convert_fusion), channel_id=1, source_target_pairs={{0,4},{1,5},{2,6},{3,7},{4,8},{5,9},{6,10},{7,11},{8,12},{9,13},{1... | collective-permute-start | bytes 1966088 | tf_op jit(solution)/shard_map/ppermute | solution.py:15
  162.0 2.8 %copy-start.3 = (f32[512,640]{1,0:T(8,128)S(1)}, f32[512,640]{1,0:T(8,128)}, u32[]{:S(2)}) copy-start(f32[512,640]{1,0:T(8,128)} %copy-done.2) | copy-start | bytes 3932164
  162.0 2.8 %copy-start.10 = (bf16[1,640,640]{1,2,0:T(8,128)(2,1)S(1)}, bf16[1,640,640]{1,2,0:T(8,128)(2,1)}, u32[]{:S(2)}) copy-start(bf16[1,640,640]{1,2,0:T(8,128)(2,1)} %all-gather.8) | copy-start | bytes 2457604
Sparse Core Ops, SparseCore 0:
  9.1 27.0 all-gather.17
  37.8 19.9 all-gather.15
  59.4 24.3 all-gather.21
  85.3 24.2 all-gather.19
  111.0 24.3 all-gather.25
  136.8 25.1 all-gather.23
where the time goes:
time: 174 us; the launch traced here: 173 us
  waiting for transfers between devices  72.5 us (42%)
  blocking collectives  41.6 us (24%)
  matrix products  20.8 us (12%)
  starting transfers between devices  14.4 us (8%)
  between operations  13.7 us (8%)
  local copies, waits for them, and re-layouts  8.03 us (5%)
  other arithmetic  2.36 us (1%)
    all_gather x3, waiting for transfers between devices, one_layer(): lax.all_gather(tap_prev, 'seqa', axis=0, tiled=True)  65.4 us
    all_gather x3, blocking collectives, one_layer(): lax.all_gather(mixing, 'seqa', axis=1, tiled=True)  41.6 us
    ppermute x3, starting transfers between devices, from_behind(): return lax.ppermute(value, axis, pairs)  14.2 us
    dot_general x3, matrix products, one_layer(): jnp.dot(earlier, lax.all_gather(tap_prev, 'seqa', axis=0, tiled=True), pr...  8.68 us
    dot_general x3, matrix products, one_layer(): jnp.dot(normed, lax.all_gather(tap_now, 'seqa', axis=0, tiled=True), pref...  8.46 us
    all_gather x3, waiting for transfers between devices, one_layer(): lax.all_gather(tap_now, 'seqa', axis=0, tiled=True)  5.31 us
    dot_general x3, matrix products, one_layer(): jnp.dot(hidden, lax.all_gather(mixing, 'seqa', axis=1, tiled=True), prefe...  3.69 us
  transfers between devices with their start and end apart: 9, of which 6 were waited for; matrix products, arithmetic and copies ran while one was open for 13% of the time, Pallas kernels for 0%

commit v1 on v0

--- a/solution.py
+++ b/solution.py
@@ -7,6 +7,19 @@
 DILATION_FIRST1 = 128
 DILATION_SECOND2 = 512
 DILATION_THIRD3 = 2048
+
+
+def rest_zones(vals, named_axis):
+    log = [vals]
+    n_chips = lax.axis_size(named_axis)
+    for it in range(1, n_chips):
+        x_new = lax.ppermute(
+            log[it - 1], axis_name=named_axis, perm=[(j, (j - 1) % n_chips) for j in range(n_chips)]
+        )
+        log.append(x_new)
+    t_next = jnp.concatenate(log, axis=0)
+    v_now = lax.axis_index(named_axis)
+    return jnp.roll(t_next, v_now * vals.shape[0], axis=0)
 
 
 def from_behind(value, axis, by):
@@ -41,9 +54,7 @@
     start_sum = jnp.broadcast_to(bias[None, :], (rows, bias.shape[0]))
     total = start_sum
     total = total + jnp.dot(
-        earlier,
-        lax.all_gather(tap_prev, "seqa", axis=0, tiled=True),
-        preferred_element_type=jnp.float32,
+        earlier, rest_zones(tap_prev, "seqa"), preferred_element_type=jnp.float32
     )
     pre = total + jnp.dot(
         normed,

time: 174 us -> 151 us (0.87)
  the two profiles are of different devices: /device:TPU:0 before, /device:TPU:1 now
where the time goes in v1:
time: 151 us
  blocking collectives  47.2 us (31%)
  waiting for transfers between devices  34.1 us (23%)
  matrix products  30.6 us (20%)
  starting transfers between devices  20.6 us (14%)
  between operations  13.3 us (9%)
  local copies, waits for them, and re-layouts  4.5 us (3%)
    all_gather x3, blocking collectives, one_layer(): lax.all_gather(mixing, 'seqa', axis=1, tiled=True)  47.2 us
    ppermute x3, waiting for transfers between devices, from_behind(): return lax.ppermute(value, axis, pairs)  20.6 us
    dot_general x3, matrix products, one_layer(): jnp.dot(earlier, rest_zones(tap_prev, 'seqa'), preferred_element_type=jnp...  19.2 us
    ppermute x9, waiting for transfers between devices, rest_zones(): lax.ppermute(log[it - 1], axis_name=named_axis, perm=[(j, (j - 1) % n_chi...  12.8 us
    ppermute x3, starting transfers between devices, from_behind(): return lax.ppermute(value, axis, pairs)  10.6 us
    ppermute x9, starting transfers between devices, rest_zones(): lax.ppermute(log[it - 1], axis_name=named_axis, perm=[(j, (j - 1) % n_chi...  9.85 us
    dot_general x3, matrix products, one_layer(): jnp.dot(normed, lax.all_gather(tap_now, 'seqa', axis=0, tiled=True), pref...  7.84 us
    dot_general x3, matrix products, one_layer(): jnp.dot(hidden, lax.all_gather(mixing, 'seqa', axis=1, tiled=True), prefe...  3.64 us
  transfers between devices with their start and end apart: 15, of which 5 were waited for; matrix products, arithmetic and copies ran while one was open for 17% of the time, Pallas kernels for 0%

profile of v1, /device:TPU:1, one launch (start us, length us, event | category | flops | bytes accessed | tf_op | source)
XLA Modules:
  0.0 151.0 jit_solution(9808023765653381087)
XLA Ops:
  6.5 2.5 %fusion.75 = (bf16[1,160,1280]{2,1,0:T(8,128)(2,1)}, bf16[1,160,1280]{2,1,0:T(8,128)(2,1)}, bf16[1,160,1280]{2,1,0:T(8,128)(2,1)}) fusion(bf16[3,160,1280]{2,1,0:T(8,128)(2,1)} %param.9), kind=kLoop, calls=%fused_computation.114 | loop fusion | bytes 2457600 | tf_op jit(solution)/shard_map/slice | solution.py:80
  9.9 1.0 slice_bitcast_fusion
  10.9 2.4 %collective-permute-start.5 = (bf16[160,1280]{1,0:T(8,128)(2,1)S(1)}, bf16[160,1280]{1,0:T(8,128)(2,1)}, u32[]{:S(2)}, u32[]{:S(2)}) collective-permute-start(bf16[160,1280]{1,0:T(8,128)(2,1)S(1)} %get-tuple-element.11), channel_id=1, source_target_pairs={{0,24},{8,0},{16,8},{24,16},{1,25},{9,1},{17,9},{25,17},{2,26},{10... | collective-permute-start | bytes 1228808 | tf_op jit(solution)/shard_map/ppermute | solution.py:16
  13.8 3.1 %collective-permute-start = (bf16[128,640]{1,0:T(8,128)(2,1)S(1)}, bf16[128,640]{1,0:T(8,128)(2,1)}, u32[]{:S(2)}, u32[]{:S(2)}) collective-permute-start(bf16[128,640]{1,0:T(8,128)(2,1)S(1)} %slice.80), channel_id=1, source_target_pairs={{0,1},{1,2},{2,3},{3,4},{4,5},{5,6},{6,7},{7,8},{8,9},{9,10},{10,1... | collective-permute-start | bytes 491528 | tf_op jit(solution)/shard_map/ppermute | solution.py:28
  16.9 1.6 %collective-permute-start.9 = (bf16[160,1280]{1,0:T(8,128)(2,1)}, bf16[160,1280]{1,0:T(8,128)(2,1)}, u32[]{:S(2)}, u32[]{:S(2)}) collective-permute-start(bf16[160,1280]{1,0:T(8,128)(2,1)} %get-tuple-element.9), channel_id=1, source_target_pairs={{0,24},{8,0},{16,8},{24,16},{1,25},{9,1},{17,9},{25,17},{2,26},{10... | collective-permute-start | bytes 1228808 | tf_op jit(solution)/shard_map/ppermute | solution.py:16
  20.4 9.2 %collective-permute-done.5 = bf16[160,1280]{1,0:T(8,128)(2,1)} collective-permute-done((bf16[160,1280]{1,0:T(8,128)(2,1)S(1)}, bf16[160,1280]{1,0:T(8,128)(2,1)}, u32[]{:S(2)}, u32[]{:S(2)}) %collective-permute-start.5) | collective-permute-done | bytes 409632 | tf_op jit(solution)/shard_map/ppermute | solution.py:16
  29.6 1.6 %collective-permute-start.6 = (bf16[160,1280]{1,0:T(8,128)(2,1)}, bf16[160,1280]{1,0:T(8,128)(2,1)}, u32[]{:S(2)}, u32[]{:S(2)}) collective-permute-start(bf16[160,1280]{1,0:T(8,128)(2,1)} %collective-permute-done.5), channel_id=1, source_target_pairs={{0,24},{8,0},{16,8},{24,16},{1,25},{9,1},{17,9},{25,17},{2,26},{10... | collective-permute-start | bytes 1228808 | tf_op jit(solution)/shard_map/ppermute | solution.py:16
  31.2 26.3 %all-gather.1 = bf16[1,640,640]{1,2,0:T(8,128)(2,1)S(1)} all-gather(bf16[1,640,160]{1,2,0:T(8,128)(2,1)S(1)} %get-tuple-element.16), channel_id=3, replica_groups=mesh['seqa'=4,'seqb'=8] {'seqa'}, dimensions={2}, use_global_device_ids=true | all-gather | bytes 1024000 | tf_op jit(solution)/shard_map/all_gather | solution.py:67
  58.0 3.4 %collective-permute-start.10 = (bf16[160,1280]{1,0:T(8,128)(2,1)}, bf16[160,1280]{1,0:T(8,128)(2,1)}, u32[]{:S(2)}, u32[]{:S(2)}) collective-permute-start(bf16[160,1280]{1,0:T(8,128)(2,1)} %collective-permute-done.9), channel_id=1, source_target_pairs={{0,24},{8,0},{16,8},{24,16},{1,25},{9,1},{17,9},{25,17},{2,26},{10... | collective-permute-start | bytes 1228808 | tf_op jit(solution)/shard_map/ppermute | solution.py:16
  61.6 2.6 %fusion.34 = f32[512,1280]{1,0:T(8,128)S(1)} fusion(bf16[512,640]{1,0:T(8,128)(2,1)S(1)} %fusion.38, bf16[1,640,1280]{2,1,0:T(8,128)(2,1)} %all-gather.10.cloned.1.call-done), kind=kOutput, calls=%fused_computation.58 | convolution fusion | flops 838860800 | bytes 4915200 | tf_op jit(solution)/shard_map/dot_general | solution.py:59
  64.2 2.7 %collective-permute-done.3 = bf16[160,1280]{1,0:T(8,128)(2,1)} collective-permute-done((bf16[160,1280]{1,0:T(8,128)(2,1)}, bf16[160,1280]{1,0:T(8,128)(2,1)}, u32[]{:S(2)}, u32[]{:S(2)}) %collective-permute-start.3) | collective-permute-done | bytes 409632 | tf_op jit(solution)/shard_map/ppermute | solution.py:16
  66.9 6.4 %fusion = f32[512,1280]{1,0:T(8,128)S(1)} fusion(f32[512,1280]{1,0:T(8,128)S(1)} %fusion.34, s32[]{:T(128)S(6)} %select_n.15, bf16[160,1280]{1,0:T(8,128)(2,1)} %get-tuple-element.10, bf16[160,1280]{1,0:T(8,128)(2,1)} %collective-permute-done.1, bf16[160,1280]{1,0:T(8,128)(2,1)} %collective-permute-done.2, bf16[160,1280]{1,0:T(8,128)(2,1)} %collective-permute-done.3, ...), kind=kOutput, calls=%fused_computation.3 | convolution fusion | flops 854589440 | bytes 7541764 | tf_op jit(solution)/shard_map/dot_general | solution.py:56
  73.3 1.0 multiply_reduce_fusion.1
  74.4 5.6 %collective-permute-start.4 = (bf16[512,640]{1,0:T(8,128)(2,1)S(1)}, bf16[512,640]{1,0:T(8,128)(2,1)S(1)}, u32[]{:S(2)}, u32[]{:S(2)}) collective-permute-start(bf16[512,640]{1,0:T(8,128)(2,1)S(1)} %multiply_convert_fusion.1), channel_id=1, source_target_pairs={{0,1},{1,2},{2,3},{3,4},{4,5},{5,6},{6,7},{7,8},{8,9},{9,10},{10,1... | collective-permute-start | bytes 1966088 | tf_op jit(solution)/shard_map/ppermute | solution.py:28
  80.0 10.6 %all-gather.3 = bf16[1,640,640]{1,2,0:T(8,128)(2,1)} all-gather(bf16[1,640,160]{1,2,0:T(8,128)(2,1)S(1)} %get-tuple-element.17), channel_id=5, replica_groups=mesh['seqa'=4,'seqb'=8] {'seqa'}, dimensions={2}, use_global_device_ids=true | all-gather | bytes 1024000 | tf_op jit(solution)/shard_map/all_gather | solution.py:67
  90.7 2.6 %fusion.32 = f32[512,1280]{1,0:T(8,128)S(1)} fusion(bf16[512,640]{1,0:T(8,128)(2,1)S(1)} %multiply_convert_fusion.1, bf16[1,640,1280]{2,1,0:T(8,128)(2,1)} %all-gather.12.cloned.1.call-done), kind=kOutput, calls=%fused_computation.56 | convolution fusion | flops 838860800 | bytes 4915200 | tf_op jit(solution)/shard_map/dot_general | solution.py:59
  93.4 2.3 %collective-permute-done.4 = bf16[512,640]{1,0:T(8,128)(2,1)S(1)} collective-permute-done((bf16[512,640]{1,0:T(8,128)(2,1)S(1)}, bf16[512,640]{1,0:T(8,128)(2,1)S(1)}, u32[]{:S(2)}, u32[]{:S(2)}) %collective-permute-start.4) | collective-permute-done | bytes 655392 | tf_op jit(solution)/shard_map/ppermute | solution.py:28
  95.7 6.3 %fusion.1 = f32[512,1280]{1,0:T(8,128)S(1)} fusion(f32[512,1280]{1,0:T(8,128)S(1)} %fusion.32, bf16[512,640]{1,0:T(8,128)(2,1)S(1)} %collective-permute-done.4, s32[]{:T(128)S(6)} %select_n.15, bf16[160,1280]{1,0:T(8,128)(2,1)S(1)} %copy-done.6, bf16[160,1280]{1,0:T(8,128)(2,1)} %collective-permute-done.5, bf16[160,1280]{1,0:T(8,128)(2,1)} %collective-permute-done.6, ...), kind=kOutput, calls=%fused_computation.4 | convolution fusion | flops 853278720 | bytes 7541764 | tf_op jit(solution)/shard_map/dot_general | solution.py:56
  103.1 1.9 %collective-permute-start.8 = (bf16[512,640]{1,0:T(8,128)(2,1)S(1)}, bf16[512,640]{1,0:T(8,128)(2,1)}, u32[]{:S(2)}, u32[]{:S(2)}) collective-permute-start(bf16[512,640]{1,0:T(8,128)(2,1)S(1)} %multiply_convert_fusion), channel_id=1, source_target_pairs={{0,4},{1,5},{2,6},{3,7},{4,8},{5,9},{6,10},{7,11},{8,12},{9,13},{1... | collective-permute-start | bytes 1966088 | tf_op jit(solution)/shard_map/ppermute | solution.py:28
  105.0 10.3 %all-gather.5 = bf16[1,640,640]{1,2,0:T(8,128)(2,1)S(1)} all-gather(bf16[1,640,160]{1,2,0:T(8,128)(2,1)S(1)} %get-tuple-element.15), channel_id=7, replica_groups=mesh['seqa'=4,'seqb'=8] {'seqa'}, dimensions={2}, use_global_device_ids=true | all-gather | bytes 1024000 | tf_op jit(solution)/shard_map/all_gather | solution.py:67
  115.3 2.6 %fusion.30 = f32[512,1280]{1,0:T(8,128)S(1)} fusion(bf16[512,640]{1,0:T(8,128)(2,1)S(1)} %multiply_convert_fusion, bf16[1,640,1280]{2,1,0:T(8,128)(2,1)} %all-gather.14.cloned.1.call-done), kind=kOutput, calls=%fused_computation.54 | convolution fusion | flops 838860800 | bytes 4915200 | tf_op jit(solution)/shard_map/dot_general | solution.py:59
  117.9 18.2 %collective-permute-done.8 = bf16[512,640]{1,0:T(8,128)(2,1)} collective-permute-done((bf16[512,640]{1,0:T(8,128)(2,1)S(1)}, bf16[512,640]{1,0:T(8,128)(2,1)}, u32[]{:S(2)}, u32[]{:S(2)}) %collective-permute-start.8) | collective-permute-done | bytes 655392 | tf_op jit(solution)/shard_map/ppermute | solution.py:28
  136.2 6.5 %fusion.2 = f32[512,1280]{1,0:T(8,128)S(1)} fusion(f32[512,1280]{1,0:T(8,128)S(1)} %fusion.30, bf16[512,640]{1,0:T(8,128)(2,1)} %collective-permute-done.8, s32[]{:T(128)S(6)} %select_n.15, bf16[160,1280]{1,0:T(8,128)(2,1)} %get-tuple-element.9, bf16[160,1280]{1,0:T(8,128)(2,1)} %collective-permute-done.9, bf16[160,1280]{1,0:T(8,128)(2,1)} %collective-permute-done.10, ...), kind=kOutput, calls=%fused_computation.5 | convolution fusion | flops 853278720 | bytes 7541764 | tf_op jit(solution)/shard_map/dot_general | solution.py:56
  142.7 1.7 %fusion.36 = bf16[512,640]{1,0:T(8,128)(2,1)} fusion(f32[512,640]{1,0:T(8,128)S(1)} %get-tuple-element.21, bf16[1,640,640]{1,2,0:T(8,128)(2,1)S(1)} %all-gather.5, f32[512,1280]{1,0:T(8,128)S(1)} %fusion.2), kind=kOutput, calls=%fused_computation.62 | convolution fusion | flops 421724160 | bytes 5406720 | tf_op jit(solution)/shard_map/dot_general | solution.py:65
  (50 shorter events, 5.2 us)
Async XLA Ops:
  6.5 3.3 %copy-start.1 = (bf16[3,160,1280]{2,1,0:T(8,128)(2,1)S(1)}, bf16[3,160,1280]{2,1,0:T(8,128)(2,1)}, u32[]{:S(2)}) copy-start(bf16[3,160,1280]{2,1,0:T(8,128)(2,1)} %param.8) | copy-start | bytes 3686404
  6.5 6.8 %copy-start = (bf16[512,640]{1,0:T(8,128)(2,1)S(1)}, bf16[512,640]{1,0:T(8,128)(2,1)}, u32[]{:S(2)}) copy-start(bf16[512,640]{1,0:T(8,128)(2,1)} %param.7) | copy-start | bytes 1966084
  6.5 55.0 %all-gather.10.cloned.1.call-start = ((), (), s32[]{:S(2)}) async-start(), calls=%async_computation | async-start | bytes 2048000 | tf_op jit(solution)/shard_map/all_gather | solution.py:61
  9.1 81.7 %all-gather.12.cloned.1.call-start = ((), (), s32[]{:S(2)}) async-start(), calls=%async_computation.1 | async-start | bytes 2048000 | tf_op jit(solution)/shard_map/all_gather | solution.py:61
  9.8 9.7 %copy-start.3 = (bf16[3,640,160]{1,2,0:T(8,128)(2,1)S(1)}, bf16[3,640,160]{1,2,0:T(8,128)(2,1)}, u32[]{:S(2)}) copy-start(bf16[3,640,160]{1,2,0:T(8,128)(2,1)} %param.11) | copy-start | bytes 1843204
  9.8 105.5 %all-gather.14.cloned.1.call-start = ((), (), s32[]{:S(2)}) async-start(), calls=%async_computation.2 | async-start | bytes 2048000 | tf_op jit(solution)/shard_map/all_gather | solution.py:61
  10.9 20.2 %copy-start.5 = (bf16[160,1280]{1,0:T(8,128)(2,1)}, bf16[160,1280]{1,0:T(8,128)(2,1)S(1)}, u32[]{:S(2)}) copy-start(bf16[160,1280]{1,0:T(8,128)(2,1)S(1)} %get-tuple-element.11) | copy-start | bytes 1228804
  10.9 8.5 %collective-permute-start.1 = (bf16[160,1280]{1,0:T(8,128)(2,1)}, bf16[160,1280]{1,0:T(8,128)(2,1)}, u32[]{:S(2)}, u32[]{:S(2)}) collective-permute-start(bf16[160,1280]{1,0:T(8,128)(2,1)} %get-tuple-element.10), channel_id=1, source_target_pairs={{0,24},{8,0},{16,8},{24,16},{1,25},{9,1},{17,9},{25,17},{2,26},{10... | collective-permute-start | bytes 1228808 | tf_op jit(solution)/shard_map/ppermute | solution.py:16
  10.9 18.6 %collective-permute-start.5 = (bf16[160,1280]{1,0:T(8,128)(2,1)S(1)}, bf16[160,1280]{1,0:T(8,128)(2,1)}, u32[]{:S(2)}, u32[]{:S(2)}) collective-permute-start(bf16[160,1280]{1,0:T(8,128)(2,1)S(1)} %get-tuple-element.11), channel_id=1, source_target_pairs={{0,24},{8,0},{16,8},{24,16},{1,25},{9,1},{17,9},{25,17},{2,26},{10... | collective-permute-start | bytes 1228808 | tf_op jit(solution)/shard_map/ppermute | solution.py:16
  13.6 44.4 %copy-start.7 = (f32[3,1280]{1,0:T(4,128)S(1)}, f32[3,1280]{1,0:T(4,128)}, u32[]{:S(2)}) copy-start(f32[3,1280]{1,0:T(4,128)} %param.10) | copy-start | bytes 46084
  13.8 50.4 %collective-permute-start = (bf16[128,640]{1,0:T(8,128)(2,1)S(1)}, bf16[128,640]{1,0:T(8,128)(2,1)}, u32[]{:S(2)}, u32[]{:S(2)}) collective-permute-start(bf16[128,640]{1,0:T(8,128)(2,1)S(1)} %slice.80), channel_id=1, source_target_pairs={{0,1},{1,2},{2,3},{3,4},{4,5},{5,6},{6,7},{7,8},{8,9},{9,10},{10,1... | collective-permute-start | bytes 491528 | tf_op jit(solution)/shard_map/ppermute | solution.py:28
  16.9 41.1 %collective-permute-start.9 = (bf16[160,1280]{1,0:T(8,128)(2,1)}, bf16[160,1280]{1,0:T(8,128)(2,1)}, u32[]{:S(2)}, u32[]{:S(2)}) collective-permute-start(bf16[160,1280]{1,0:T(8,128)(2,1)} %get-tuple-element.9), channel_id=1, source_target_pairs={{0,24},{8,0},{16,8},{24,16},{1,25},{9,1},{17,9},{25,17},{2,26},{10... | collective-permute-start | bytes 1228808 | tf_op jit(solution)/shard_map/ppermute | solution.py:16
  19.5 38.0 %collective-permute-start.2 = (bf16[160,1280]{1,0:T(8,128)(2,1)}, bf16[160,1280]{1,0:T(8,128)(2,1)}, u32[]{:S(2)}, u32[]{:S(2)}) collective-permute-start(bf16[160,1280]{1,0:T(8,128)(2,1)} %collective-permute-done.1), channel_id=1, source_target_pairs={{0,24},{8,0},{16,8},{24,16},{1,25},{9,1},{17,9},{25,17},{2,26},{10... | collective-permute-start | bytes 1228808 | tf_op jit(solution)/shard_map/ppermute | solution.py:16
  29.6 31.8 %collective-permute-start.6 = (bf16[160,1280]{1,0:T(8,128)(2,1)}, bf16[160,1280]{1,0:T(8,128)(2,1)}, u32[]{:S(2)}, u32[]{:S(2)}) collective-permute-start(bf16[160,1280]{1,0:T(8,128)(2,1)} %collective-permute-done.5), channel_id=1, source_target_pairs={{0,24},{8,0},{16,8},{24,16},{1,25},{9,1},{17,9},{25,17},{2,26},{10... | collective-permute-start | bytes 1228808 | tf_op jit(solution)/shard_map/ppermute | solution.py:16
  57.4 9.4 %collective-permute-start.3 = (bf16[160,1280]{1,0:T(8,128)(2,1)}, bf16[160,1280]{1,0:T(8,128)(2,1)}, u32[]{:S(2)}, u32[]{:S(2)}) collective-permute-start(bf16[160,1280]{1,0:T(8,128)(2,1)} %collective-permute-done.2), channel_id=1, source_target_pairs={{0,24},{8,0},{16,8},{24,16},{1,25},{9,1},{17,9},{25,17},{2,26},{10... | collective-permute-start | bytes 1228808 | tf_op jit(solution)/shard_map/ppermute | solution.py:16
  58.0 8.9 %copy-start.4 = (bf16[384,640]{1,0:T(8,128)(2,1)S(1)}, bf16[384,640]{1,0:T(8,128)(2,1)}, u32[]{:S(2)}) copy-start(bf16[384,640]{1,0:T(8,128)(2,1)} %slice.81) | copy-start | bytes 1474564
  58.0 32.6 %collective-permute-start.10 = (bf16[160,1280]{1,0:T(8,128)(2,1)}, bf16[160,1280]{1,0:T(8,128)(2,1)}, u32[]{:S(2)}, u32[]{:S(2)}) collective-permute-start(bf16[160,1280]{1,0:T(8,128)(2,1)} %collective-permute-done.9), channel_id=1, source_target_pairs={{0,24},{8,0},{16,8},{24,16},{1,25},{9,1},{17,9},{25,17},{2,26},{10... | collective-permute-start | bytes 1228808 | tf_op jit(solution)/shard_map/ppermute | solution.py:16
  61.4 32.0 %collective-permute-start.7 = (bf16[160,1280]{1,0:T(8,128)(2,1)}, bf16[160,1280]{1,0:T(8,128)(2,1)}, u32[]{:S(2)}, u32[]{:S(2)}) collective-permute-start(bf16[160,1280]{1,0:T(8,128)(2,1)} %collective-permute-done.6), channel_id=1, source_target_pairs={{0,24},{8,0},{16,8},{24,16},{1,25},{9,1},{17,9},{25,17},{2,26},{10... | collective-permute-start | bytes 1228808 | tf_op jit(solution)/shard_map/ppermute | solution.py:16
  74.4 21.3 %collective-permute-start.4 = (bf16[512,640]{1,0:T(8,128)(2,1)S(1)}, bf16[512,640]{1,0:T(8,128)(2,1)S(1)}, u32[]{:S(2)}, u32[]{:S(2)}) collective-permute-start(bf16[512,640]{1,0:T(8,128)(2,1)S(1)} %multiply_convert_fusion.1), channel_id=1, source_target_pairs={{0,1},{1,2},{2,3},{3,4},{4,5},{5,6},{6,7},{7,8},{8,9},{9,10},{10,1... | collective-permute-start | bytes 1966088 | tf_op jit(solution)/shard_map/ppermute | solution.py:28
  90.6 5.1 %copy-start.6 = (bf16[160,1280]{1,0:T(8,128)(2,1)S(1)}, bf16[160,1280]{1,0:T(8,128)(2,1)}, u32[]{:S(2)}) copy-start(bf16[160,1280]{1,0:T(8,128)(2,1)} %copy-done.5) | copy-start | bytes 1228804
  90.6 27.4 %collective-permute-start.11 = (bf16[160,1280]{1,0:T(8,128)(2,1)}, bf16[160,1280]{1,0:T(8,128)(2,1)}, u32[]{:S(2)}, u32[]{:S(2)}) collective-permute-start(bf16[160,1280]{1,0:T(8,128)(2,1)} %collective-permute-done.10), channel_id=1, source_target_pairs={{0,24},{8,0},{16,8},{24,16},{1,25},{9,1},{17,9},{25,17},{2,26},{10... | collective-permute-start | bytes 1228808 | tf_op jit(solution)/shard_map/ppermute | solution.py:16
  95.7 6.3 %copy-start.2 = (bf16[1,640,640]{1,2,0:T(8,128)(2,1)S(1)}, bf16[1,640,640]{1,2,0:T(8,128)(2,1)}, u32[]{:S(2)}) copy-start(bf16[1,640,640]{1,2,0:T(8,128)(2,1)} %all-gather.3) | copy-start | bytes 2457604
  103.1 33.1 %collective-permute-start.8 = (bf16[512,640]{1,0:T(8,128)(2,1)S(1)}, bf16[512,640]{1,0:T(8,128)(2,1)}, u32[]{:S(2)}, u32[]{:S(2)}) collective-permute-start(bf16[512,640]{1,0:T(8,128)(2,1)S(1)} %multiply_convert_fusion), channel_id=1, source_target_pairs={{0,4},{1,5},{2,6},{3,7},{4,8},{5,9},{6,10},{7,11},{8,12},{9,13},{1... | collective-permute-start | bytes 1966088 | tf_op jit(solution)/shard_map/ppermute | solution.py:28
Sparse Core Ops, SparseCore 0:
  9.2 26.9 all-gather.9
  37.7 22.9 all-gather.11
  62.3 24.6 all-gather.13
